TPU v7x, 32 devices: a whole 2x2x4 slice. The times are simulated.
32 devices in a mesh: shard: 4 (over y, x), replica: 8 (over z, core).
Axes of the slice: x: 2, y: 2, z: 4, core: 2. Of those that a mesh axis runs over, the one named last changes fastest.
Arguments:
- hidden_in: bfloat16 [32, 212, 960], P(('shard', 'replica')), may hold values from -9 to 9
- cotangent: bfloat16 [32, 212, 960], P(('shard', 'replica')), may hold values from -6 to 6
- segment_ids: int32 [32, 212], P(('shard', 'replica')), may hold values from 0 to 6, as said below
- positions: int32 [32, 212], P(('shard', 'replica')), may hold values from 0 to 211, as said below
- w_qkv: bfloat16 [960, 1600], P(None, 'shard'), may hold values from -1 to 1
- w_out: bfloat16 [960, 960], P(None, 'shard'), may hold values from -0.5 to 0.5
- w_gate: bfloat16 [960, 2560], P(None, 'shard'), may hold values from -0.1875 to 0.1875
- w_up: bfloat16 [960, 2560], P(None, 'shard'), may hold values from -0.1875 to 0.1875
- w_down: bfloat16 [2560, 960], P('shard'), may hold values from -0.25 to 0.25
- gain_attn: bfloat16 [960], P('shard'), may hold values from 0.5 to 1.5
- gain_mlp: bfloat16 [960], P('shard'), may hold values from 0.5 to 1.5
Outputs:
- hidden_out: bfloat16 [32, 212, 960], P(('shard', 'replica'))
- grad_input: float32 [32, 212, 960], P(('shard', 'replica'))
- grad_qkv: float32 [960, 1600], P(None, 'shard')
- grad_out: float32 [960, 960], P(None, 'shard')
- grad_gate: float32 [960, 2560], P(None, 'shard')
- grad_up: float32 [960, 2560], P(None, 'shard')
- grad_down: float32 [2560, 960], P('shard')
- grad_gain_attn: float32 [960], P('shard')
- grad_gain_mlp: float32 [960], P('shard')
Inputs may be any that keep to these rules, and one draw needn't show every extreme that they name: `segment_ids`: within each sequence the numbers start at 0 and never fall; a run of equal numbers is one document. `positions`: the offset of each token from the first token of its document.
All inputs are finite; a program needn't handle non-finite values.
Results may differ from a plain program's by a relative error of at most 0.022.
Values may be sent and summed in bfloat16 or wider, within the bound.
A program may use at most 128 MiB of HBM per device.

v0:
```python
import math
import jax
import jax.numpy as jnp
from jax import lax
from jax.sharding import PartitionSpec as P

D = 960
H = 15
KV = 5
HD = 64
LEN = 212
EPSILON = 1e-05
THETA_BASE = 100000.0
NEG_FILL = -1e30


def rope_tables(position_ids):
    half_width = HD // 2
    freq_steps = jnp.arange(half_width, dtype=jnp.float32) * (2.0 / HD)
    inverse = jnp.exp(-math.log(THETA_BASE) * freq_steps)
    angles = position_ids.astype(jnp.float32)[:, None] * inverse[None, :]
    cosine = jnp.cos(angles)
    sine_part = jnp.sin(angles)
    return (jnp.concatenate([cosine, cosine], -1), jnp.concatenate([sine_part, sine_part], -1))


def rotate(tensor, cosine, sine_part):
    half_width = HD // 2
    turned = jnp.concatenate([-tensor[..., half_width:], tensor[..., :half_width]], -1)
    return tensor * cosine[:, None, :] + turned * sine_part[:, None, :]


def rotate_back(gradient, cosine, sine_part):
    half_width = HD // 2
    scaled = gradient * sine_part[:, None, :]
    return gradient * cosine[:, None, :] + jnp.concatenate(
        [scaled[..., half_width:], -scaled[..., :half_width]], -1
    )


def norm_forward(values, gain_row):
    inv_rms = lax.rsqrt(jnp.mean(values * values, -1, keepdims=True) + EPSILON)
    return ((values * inv_rms * gain_row.astype(jnp.float32)).astype(jnp.bfloat16), inv_rms)


def norm_backward(values, inv_rms, gain_row, grad_normed):
    weighted = grad_normed * gain_row.astype(jnp.float32)
    gain_grad = jnp.sum(grad_normed * values * inv_rms, 0)
    inner_mean = jnp.mean(weighted * values, -1, keepdims=True)
    return (inv_rms * weighted - values * inv_rms**3 * inner_mean, gain_grad)


def silu_parts(gate_pre):
    sigmoid_val = jax.nn.sigmoid(gate_pre)
    return (gate_pre * sigmoid_val, sigmoid_val * (1.0 + gate_pre * (1.0 - sigmoid_val)))


def attention_forward(queries, keys_in, values_in, allowed):
    length = queries.shape[0]
    groups = H // KV
    scale_factor = HD ** (-0.5)
    query_g = queries.reshape(length, KV, groups, HD)
    scores = (
        jnp.einsum("qkgd,skd->kgqs", query_g, keys_in, preferred_element_type=jnp.float32)
        * scale_factor
    )
    scores = jnp.where(allowed, scores, NEG_FILL)
    highest = jnp.max(scores, -1, keepdims=True)
    raw_weights = jnp.exp(scores - highest)
    totals = jnp.sum(raw_weights, -1, keepdims=True)
    log_total = highest + jnp.log(totals)
    attn_probs = (raw_weights / totals).astype(jnp.bfloat16)
    mixed_vals = jnp.einsum(
        "kgqs,skd->qkgd", attn_probs, values_in, preferred_element_type=jnp.float32
    )
    return (mixed_vals.reshape(length, H * HD).astype(jnp.bfloat16), log_total)


def attention_backward(queries, keys_in, values_in, allowed, log_total, attended, grad_attended):
    length = queries.shape[0]
    groups = H // KV
    scale_factor = HD ** (-0.5)
    query_g = queries.reshape(length, KV, groups, HD)
    scores = (
        jnp.einsum("qkgd,skd->kgqs", query_g, keys_in, preferred_element_type=jnp.float32)
        * scale_factor
    )
    scores = jnp.where(allowed, scores, NEG_FILL)
    attn_probs = jnp.exp(scores - log_total)
    probs_b = attn_probs.astype(jnp.bfloat16)
    grad_g = grad_attended.reshape(length, KV, groups, HD)
    attended_g = attended.reshape(length, KV, groups, HD)
    grad_values = jnp.einsum("kgqs,qkgd->skd", probs_b, grad_g, preferred_element_type=jnp.float32)
    grad_probs = jnp.einsum("qkgd,skd->kgqs", grad_g, values_in, preferred_element_type=jnp.float32)
    delta_row = jnp.sum(grad_g.astype(jnp.float32) * attended_g.astype(jnp.float32), -1)
    delta_row = jnp.transpose(delta_row, (1, 2, 0))[..., None]
    grad_scores = (attn_probs * (grad_probs - delta_row) * scale_factor).astype(jnp.bfloat16)
    grad_queries = jnp.einsum(
        "kgqs,skd->qkgd", grad_scores, keys_in, preferred_element_type=jnp.float32
    ).reshape(length, H, HD)
    grad_keys = jnp.einsum(
        "kgqs,qkgd->skd", grad_scores, query_g, preferred_element_type=jnp.float32
    )
    return (grad_queries, grad_keys, grad_values)


def on_device(
    hidden_in,
    cotangent,
    segment_ids,
    positions,
    w_qkv,
    w_out,
    w_gate,
    w_up,
    w_down,
    gain_attn,
    gain_mlp,
):
    row_total = hidden_in.shape[0] * LEN
    in_rows = hidden_in.reshape(row_total, D)
    flat_rows = in_rows.astype(jnp.float32)
    segment_row = segment_ids.reshape(row_total)
    row_index = jnp.arange(row_total)
    sequence_of = row_index // LEN
    allowed = (
        (sequence_of[:, None] == sequence_of[None, :])
        & (segment_row[:, None] == segment_row[None, :])
        & (row_index[None, :] <= row_index[:, None])
    )
    cosine, sine_part = rope_tables(positions.reshape(row_total))
    full_qkv, full_out, gain_a, gain_m = (
        lax.all_gather(w_qkv, "shard", axis=1, tiled=True),
        lax.all_gather(w_out, "shard", axis=1, tiled=True),
        lax.all_gather(gain_attn, "shard", axis=0, tiled=True),
        lax.all_gather(gain_mlp, "shard", axis=0, tiled=True),
    )
    normed_one, inv_one = norm_forward(flat_rows, gain_a)
    projected = jnp.dot(normed_one, full_qkv, preferred_element_type=jnp.float32)
    queries = rotate(projected[:, : H * HD].reshape(row_total, H, HD), cosine, sine_part).astype(
        jnp.bfloat16
    )
    keys_b = rotate(
        projected[:, H * HD : (H + KV) * HD].reshape(row_total, KV, HD), cosine, sine_part
    ).astype(jnp.bfloat16)
    values_b = projected[:, (H + KV) * HD :].reshape(row_total, KV, HD).astype(jnp.bfloat16)
    attended, log_total = attention_forward(queries, keys_b, values_b, allowed)
    middle = flat_rows + jnp.dot(attended, full_out, preferred_element_type=jnp.float32)
    normed_two, inv_two = norm_forward(middle, gain_m)
    group_rows = lax.all_gather(normed_two, "shard", axis=0, tiled=True)
    gate_pre = jnp.dot(group_rows, w_gate, preferred_element_type=jnp.float32)
    up_pre = jnp.dot(group_rows, w_up, preferred_element_type=jnp.float32)
    silu_val, silu_slope = silu_parts(gate_pre)
    activated = (silu_val * up_pre).astype(jnp.bfloat16)
    branch_out = lax.psum_scatter(
        jnp.dot(activated, w_down, preferred_element_type=jnp.float32).astype(jnp.bfloat16),
        "shard",
        scatter_dimension=0,
        tiled=True,
    ).astype(jnp.float32)
    hidden_out = (middle + branch_out).astype(jnp.bfloat16).reshape(hidden_in.shape)
    cot_rows = cotangent.reshape(row_total, D)
    cot_float = cot_rows.astype(jnp.float32)
    group_cot = lax.all_gather(cot_rows, "shard", axis=0, tiled=True)
    grad_act = jnp.dot(group_cot, w_down.T, preferred_element_type=jnp.float32)
    grad_up_b = (grad_act * silu_val).astype(jnp.bfloat16)
    grad_gate_b = (grad_act * up_pre * silu_slope).astype(jnp.bfloat16)
    own_down = jnp.dot(activated.T, group_cot, preferred_element_type=jnp.float32)
    own_gate = jnp.dot(group_rows.T, grad_gate_b, preferred_element_type=jnp.float32)
    own_up = jnp.dot(group_rows.T, grad_up_b, preferred_element_type=jnp.float32)
    grad_normed = lax.psum_scatter(
        (
            jnp.dot(grad_gate_b, w_gate.T, preferred_element_type=jnp.float32)
            + jnp.dot(grad_up_b, w_up.T, preferred_element_type=jnp.float32)
        ).astype(jnp.bfloat16),
        "shard",
        scatter_dimension=0,
        tiled=True,
    ).astype(jnp.float32)
    back_two, gain_two_grad = norm_backward(middle, inv_two, gain_m, grad_normed)
    grad_middle = cot_float + back_two
    grad_middle_b = grad_middle.astype(jnp.bfloat16)
    again_qkv, again_out = (
        lax.all_gather(w_qkv, "shard", axis=1, tiled=True),
        lax.all_gather(w_out, "shard", axis=1, tiled=True),
    )
    grad_attended = jnp.dot(grad_middle_b, again_out.T, preferred_element_type=jnp.float32).astype(
        jnp.bfloat16
    )
    grad_queries, grad_keys, grad_values = attention_backward(
        queries, keys_b, values_b, allowed, log_total, attended, grad_attended
    )
    grad_queries = rotate_back(grad_queries, cosine, sine_part)
    grad_keys = rotate_back(grad_keys, cosine, sine_part)
    grad_proj = jnp.concatenate(
        [
            grad_queries.reshape(row_total, H * HD),
            grad_keys.reshape(row_total, KV * HD),
            grad_values.reshape(row_total, KV * HD),
        ],
        1,
    ).astype(jnp.bfloat16)
    grad_normed_one = jnp.dot(grad_proj, again_qkv.T, preferred_element_type=jnp.float32)
    back_one, gain_one_grad = norm_backward(flat_rows, inv_one, gain_a, grad_normed_one)
    grad_input = (grad_middle + back_one).reshape(hidden_in.shape)
    own_qkv, own_out, own_gain_a, own_gain_m = (
        lax.psum_scatter(
            jnp.dot(normed_one.T, grad_proj, preferred_element_type=jnp.float32).astype(
                jnp.bfloat16
            ),
            "shard",
            scatter_dimension=1,
            tiled=True,
        ).astype(jnp.float32),
        lax.psum_scatter(
            jnp.dot(attended.T, grad_middle_b, preferred_element_type=jnp.float32).astype(
                jnp.bfloat16
            ),
            "shard",
            scatter_dimension=1,
            tiled=True,
        ).astype(jnp.float32),
        lax.psum_scatter(
            gain_one_grad.astype(jnp.bfloat16), "shard", scatter_dimension=0, tiled=True
        ).astype(jnp.float32),
        lax.psum_scatter(
            gain_two_grad.astype(jnp.bfloat16), "shard", scatter_dimension=0, tiled=True
        ).astype(jnp.float32),
    )
    summed = (
        lax.psum(own_qkv.astype(jnp.bfloat16), "replica").astype(jnp.float32),
        lax.psum(own_out.astype(jnp.bfloat16), "replica").astype(jnp.float32),
        lax.psum(own_gate.astype(jnp.bfloat16), "replica").astype(jnp.float32),
        lax.psum(own_up.astype(jnp.bfloat16), "replica").astype(jnp.float32),
        lax.psum(own_down.astype(jnp.bfloat16), "replica").astype(jnp.float32),
        lax.psum(own_gain_a.astype(jnp.bfloat16), "replica").astype(jnp.float32),
        lax.psum(own_gain_m.astype(jnp.bfloat16), "replica").astype(jnp.float32),
    )
    return (
        hidden_out,
        grad_input,
        summed[0],
        summed[1],
        summed[2],
        summed[3],
        summed[4],
        summed[5],
        summed[6],
    )


def solution(mesh):
    in_specs = (
        P(("shard", "replica"), None, None),
        P(("shard", "replica"), None, None),
        P(("shard", "replica"), None),
        P(("shard", "replica"), None),
        P(None, "shard"),
        P(None, "shard"),
        P(None, "shard"),
        P(None, "shard"),
        P("shard", None),
        P("shard"),
        P("shard"),
    )
    out_specs = (
        P(("shard", "replica"), None, None),
        P(("shard", "replica"), None, None),
        P(None, "shard"),
        P(None, "shard"),
        P(None, "shard"),
        P(None, "shard"),
        P("shard", None),
        P("shard"),
        P("shard"),
    )
    return jax.shard_map(
        on_device, mesh=mesh, in_specs=in_specs, out_specs=out_specs, check_vma=False
    )
```

profile of v0, /device:TPU:0, one launch (start us, length us, event | category | flops | bytes accessed | tf_op | source)
XLA Modules:
  0.0 492.3 jit_solution(3452470993920954828)
XLA Ops:
  7.3 0.7 all-gather.7.cloned.1.call-update
  8.0 2.1 copy.61
  10.2 1.6 copy.62
  13.8 11.5 %all-reduce.11 = (bf16[960]{0:T(1024)(128)(2,1)S(1)}, bf16[960]{0:T(1024)(128)(2,1)S(1)}) all-reduce(bf16[960]{0:T(1024)(128)(2,1)S(1)} %dynamic-update-slice, bf16[960]{0:T(1024)(128)(2,1)S(1)} %dynamic-update-slice.1), channel_id=1, replica_groups=mesh['shard'=4,'replica'=8] {'shard'}, use_global_device_ids=true, to_apply=%add | all-reduce | flops 1920 | bytes 7680
  25.5 0.6 pad_maximum_fusion.4
  26.8 0.7 fusion.55
  27.5 30.0 %all-gather.7.cloned.1.call-done = bf16[960,1600]{0,1:T(8,128)(2,1)} async-done(((bf16[960,400]{0,1:T(8,128)(2,1)}), bf16[960,1600]{0,1:T(8,128)(2,1)}) %all-gather.7.cloned.1.call-update) | async-done | bytes 3072016 | tf_op jit(solution)/shard_map/all_gather | solution.py:133
  57.5 3.2 fusion.58
  61.0 0.8 copy.56
  61.8 0.9 copy.57
  63.1 1.1 slice_negate_fusion.3
  64.1 1.1 fusion.56
  66.1 0.7 fusion.68
  67.4 1.3 copy-done.2
  68.7 0.7 fusion.19
  69.4 24.7 %all-gather.9.cloned.1.call-done = bf16[960,960]{0,1:T(8,128)(2,1)} async-done(((bf16[960,240]{0,1:T(8,128)(2,1)}), bf16[960,960]{0,1:T(8,128)(2,1)}) %all-gather.9.cloned.1.call-update) | async-done | bytes 1843216 | tf_op jit(solution)/shard_map/all_gather | solution.py:134
  94.1 2.4 multiply_reduce_fusion.1
  96.5 0.9 fusion.47
  97.7 45.5 %all-gather.11.cloned.1.call-done = bf16[1,848,960]{2,0,1:T(2,128)(2,1)} async-done(((bf16[1,212,960]{2,0,1:T(2,128)(2,1)}), bf16[1,848,960]{2,0,1:T(2,128)(2,1)}) %all-gather.11.cloned.1.call-update) | async-done | bytes 1628176 | tf_op jit(solution)/shard_map/all_gather | solution.py:164
  143.2 9.4 %copy.63 = bf16[1,848,960]{1,2,0:T(8,128)(2,1)} copy(bf16[1,848,960]{2,0,1:T(2,128)(2,1)} %all-gather.11.cloned.1.call-done) | data formatting | bytes 3256320 | tf_op jit(solution)/shard_map/all_gather | solution.py:164
  152.6 25.4 %all-gather.13.cloned.1.call-done = bf16[4,212,960]{2,1,0:T(8,128)(2,1)} async-done(((bf16[1,212,960]{2,1,0:T(8,128)(2,1)}), bf16[4,212,960]{2,1,0:T(8,128)(2,1)}) %all-gather.13.cloned.1.call-update) | async-done | bytes 1628176 | tf_op jit(solution)/shard_map/all_gather | solution.py:150
  177.9 2.8 reshape.177
  180.7 3.5 fusion.70
  184.2 1.5 fusion.69
  185.8 2.4 multiply_convert_fusion
  188.2 2.7 convolution_convert_fusion.2
  190.9 1.5 fusion.71
  192.5 2.7 add_convert_fusion
  195.3 65.1 %fusion.64 = (bf16[224,960]{1,0:T(8,128)(2,1)S(1)}, bf16[224,960]{1,0:T(8,128)(2,1)S(1)}) fusion(bf16[848,960]{1,0:T(8,128)(2,1)} %convolution_convert_fusion.2, bf16[848,960]{1,0:T(8,128)(2,1)} %add_convert_fusion), kind=kCustom, calls=%all-reduce-scatter.2 | all-reduce-scatter fusion | flops 1720321 | bytes 4116992
  260.4 2.4 collective-permute-start.1
  263.5 4.3 collective-permute-start
  267.8 0.9 concatenate.40
  269.1 0.7 collective-permute-done
  269.8 0.8 concatenate.39
  270.7 2.6 fusion.33
  273.3 1.8 convolution_convert_fusion.1
  275.1 2.4 copy.77
  277.8 3.4 convolution_convert_fusion.5
  281.2 2.0 copy.64
  283.2 1.4 multiply_reduce_fusion
  284.6 2.2 fusion.4
  287.6 0.9 copy-done.9
  288.5 0.7 broadcast_multiply_fusion
  289.7 0.7 fusion.23
  290.4 0.7 copy-done.28
  291.0 2.9 convolution_convert_fusion
  294.0 1.4 copy-done.15
  295.4 4.0 fusion.16
  299.4 2.7 convolution_convert_fusion.3
  302.1 2.7 convolution_convert_fusion.4
  304.9 7.9 %reduce-scatter.11.cloned.1.call-done = bf16[240,960]{1,0:T(8,128)(2,1)} async-done(((bf16[960,960]{1,0:T(8,128)(2,1)}), bf16[240,960]{1,0:T(8,128)(2,1)}) %reduce-scatter.11.cloned.1.call-update) | async-done | bytes 460816
  312.8 2.0 copy.78
  314.8 45.9 %reduce-scatter.9.cloned.1.call-done = bf16[960,400]{0,1:T(8,128)(2,1)} async-done(((bf16[960,1600]{0,1:T(8,128)(2,1)}), bf16[960,400]{0,1:T(8,128)(2,1)}) %reduce-scatter.9.cloned.1.call-update) | async-done | bytes 768016 | tf_op jit(solution)/shard_map/reduce_scatter | solution.py:207
  361.9 3.1 fusion.46
  365.0 8.9 %all-reduce.10 = (bf16[960]{0:T(1024)(128)(2,1)S(1)}, bf16[960]{0:T(1024)(128)(2,1)S(1)}) all-reduce(bf16[960]{0:T(1024)(128)(2,1)S(1)} %get-tuple-element.47, bf16[960]{0:T(1024)(128)(2,1)S(1)} %get-tuple-element.45), channel_id=7, replica_groups=mesh['shard'=4,'replica'=8] {'shard'}, use_global_device_ids=true, to_apply=%region_17.18.clone | all-reduce | flops 1920 | bytes 7680
  374.1 15.1 %all-reduce.8 = (bf16[240]{0:T(256)(128)(2,1)S(1)}, bf16[240]{0:T(256)(128)(2,1)S(1)}) all-reduce(bf16[240]{0:T(256)(128)(2,1)S(1)} %dynamic-slice.7, bf16[240]{0:T(256)(128)(2,1)S(1)} %dynamic-slice.9), channel_id=1, replica_groups=mesh['shard'=4,'replica'=8] {'replica'}, use_global_device_ids=true, to_apply=%region_18.19 | all-reduce | flops 480 | bytes 1920 | tf_op jit(solution)/shard_map/psum | solution.py:236
  390.3 1.4 fusion.43
  391.8 1.8 copy.68
  393.6 83.1 %all-reduce.15.cloned.1.call-done = (bf16[960,400]{0,1:T(8,128)(2,1)}, bf16[960,240]{1,0:T(8,128)(2,1)}, bf16[960,640]{1,0:T(8,128)(2,1)}, bf16[960,640]{1,0:T(8,128)(2,1)}, bf16[640,960]{0,1:T(8,128)(2,1)}) async-done(((bf16[960,400]{0,1:T(8,128)(2,1)}, bf16[960,240]{1,0:T(8,128)(2,1)}, bf16[960,640]{1,0:T(8,128)(2,1)}, bf16[960,640]{1,0:T(8,128)(2,1)}, bf16[640,960]{0,1:T(8,128)(2,1)}), ...) | async-done | bytes 4915216 | tf_op jit(solution)/shard_map/psum | solution.py:231
  476.7 2.6 convert_element_type.183
  479.4 1.0 convert_element_type.185
  480.4 1.6 convert_element_type.187
  482.1 1.6 convert_element_type.189
  483.9 1.6 convert_element_type.191
  (137 shorter events, 9.0 us)
Async XLA Ops:
  7.2 178.6 %copy-start = (bf16[640,960]{0,1:T(8,128)(2,1)S(1)}, bf16[640,960]{0,1:T(8,128)(2,1)}, u32[]{:S(2)}) copy-start(bf16[640,960]{0,1:T(8,128)(2,1)} %param.19) | copy-start | bytes 3686404
  7.2 3.0 copy-start.11
  7.2 50.3 %all-gather.7.cloned.1.call-start = ((), (), s32[]{:S(2)}) async-start(), calls=%async_computation.2 | async-start | bytes 4096000 | tf_op jit(solution)/shard_map/all_gather | solution.py:133
  7.9 3.9 copy-start.34
  7.9 3.9 copy-start.5
  8.0 86.2 %all-gather.9.cloned.1.call-start = ((), (), s32[]{:S(2)}) async-start(), calls=%async_computation.3 | async-start | bytes 2457600 | tf_op jit(solution)/shard_map/all_gather | solution.py:134
  10.1 2.0 copy-start.32
  10.1 3.3 copy-start.37
  10.1 3.5 copy-start.38
  10.1 16.7 %copy-start.33 = (s32[1,212]{1,0:T(1,128)S(1)}, s32[1,212]{1,0:T(1,128)}, u32[]{:S(2)}) copy-start(s32[1,212]{1,0:T(1,128)} %param.13) | copy-start | bytes 2548
  10.1 133.1 %all-gather.11.cloned.1.call-start = ((), (), s32[]{:S(2)}) async-start(), calls=%async_computation.5 | async-start | bytes 4341760 | tf_op jit(solution)/shard_map/all_gather | solution.py:164
  11.8 166.2 %all-gather.13.cloned.1.call-start = ((), (), s32[]{:S(2)}) async-start(), calls=%async_computation.6 | async-start | bytes 2211840 | tf_op jit(solution)/shard_map/all_gather | solution.py:150
  63.0 2.3 copy-start.16
  63.0 2.3 copy-start.17
  65.2 0.7 copy-start.18
  65.3 0.8 copy-start.27
  66.1 0.8 copy-start.8
  66.9 1.8 copy-start.2
  66.9 1.8 copy-start.23
  69.4 203.8 %copy-start.10 = (bf16[5,64,3,212]{3,1,2,0:T(8,128)(2,1)}, bf16[5,64,3,212]{3,1,2,0:T(8,128)(2,1)S(1)}, u32[]{:S(2)}) copy-start(bf16[5,64,3,212]{3,1,2,0:T(8,128)(2,1)S(1)} %fusion.19) | copy-start | bytes 1221124
  97.5 215.3 %reduce-scatter.11.cloned.1.call-start = ((), (), s32[]{:S(2)}) async-start(), calls=%async_computation.7 | async-start | bytes 2457600
  180.7 3.5 copy-start.12
  180.7 3.5 copy-start.35
  184.2 1.5 copy-start.14
  188.2 2.8 copy-start.43
  188.2 2.8 copy-start.41
  188.2 4.3 copy-start.39
  190.9 1.6 copy-start.36
  260.4 7.4 %collective-permute-start.1 = (bf16[36,960]{1,0:T(8,128)(2,1)S(1)}, bf16[36,960]{1,0:T(8,128)(2,1)S(1)}, u32[]{:S(2)}, u32[]{:S(2)}) collective-permute-start(bf16[36,960]{1,0:T(8,128)(2,1)S(1)} %slice.57), channel_id=1, source_target_pairs={{0,8},{8,16},{16,24},{1,9},{9,17},{17,25},{2,10},{10,18},{18,26},{... | collective-permute-start | bytes 207368
  263.5 6.3 %collective-permute-start = (bf16[36,960]{1,0:T(8,128)(2,1)S(1)}, bf16[36,960]{1,0:T(8,128)(2,1)S(1)}, u32[]{:S(2)}, u32[]{:S(2)}) collective-permute-start(bf16[36,960]{1,0:T(8,128)(2,1)S(1)} %slice.56), channel_id=1, source_target_pairs={{0,8},{8,16},{16,24},{1,9},{9,17},{17,25},{2,10},{10,18},{18,26},{... | collective-permute-start | bytes 207368
  277.5 83.1 %reduce-scatter.9.cloned.1.call-start = ((), (), s32[]{:S(2)}) async-start(), calls=%async_computation.4 | async-start | bytes 4096000 | tf_op jit(solution)/shard_map/reduce_scatter | solution.py:207
  277.8 6.7 %copy-start.3 = (f32[5,3,212,212]{2,3,1,0:T(8,128)S(1)}, f32[5,3,212,212]{2,3,1,0:T(8,128)}, u32[]{:S(2)}) copy-start(f32[5,3,212,212]{2,3,1,0:T(8,128)} %copy-done.2) | copy-start | bytes 8089924
  284.5 2.2 copy-start.19
  287.5 1.0 copy-start.9
  288.5 1.9 copy-start.24
  288.5 1.2 copy-start.4
  289.7 0.7 copy-start.30
  289.7 1.3 copy-start.6
  290.4 0.7 copy-start.28
  293.9 1.5 copy-start.15
  294.0 5.4 %copy-start.13 = (bf16[848,960]{1,0:T(8,128)(2,1)S(1)}, bf16[848,960]{1,0:T(8,128)(2,1)}, u32[]{:S(2)}) copy-start(bf16[848,960]{1,0:T(8,128)(2,1)} %reshape.177) | copy-start | bytes 4884484
  294.0 182.8 %all-reduce.15.cloned.1.call-start = ((), (), s32[]{:S(2)}) async-start(), calls=%async_computation.8 | async-start | bytes 9994240 | tf_op jit(solution)/shard_map/psum | solution.py:231
  295.4 4.0 copy-start.40
  299.4 2.7 copy-start.42
  360.7 1.0 copy-start.7
  360.7 1.2 copy-start.25
  360.7 1.2 copy-start.29
  360.7 1.3 copy-start.31
  476.7 2.6 copy-start.26
  476.7 3.6 copy-start.22
  480.4 1.8 copy-start.21
  482.1 1.8 copy-start.20
  483.7 1.8 copy-start.1
Sparse Core Ops, SparseCore 0:
  9.9 47.6 all-gather.6
  60.0 34.1 all-gather.8
  96.5 46.5 all-gather.10
  145.4 32.4 all-gather.12
  277.6 35.0 reduce-scatter.10
  315.6 44.9 reduce-scatter.8
  364.0 112.6 all-reduce.14
where the time goes:
time: 494 us; the launch traced here: 492 us
  waiting for transfers between devices  264 us (53%)
  blocking collectives  101 us (20%)
  matrix products  46 us (9%)
  local copies, waits for them, and re-layouts  35.4 us (7%)
  other arithmetic  22.2 us (4%)
  between operations  16.8 us (3%)
  starting transfers between devices  7.37 us (1%)
    unnamed x3, blocking collectives  85.5 us
    psum x1, waiting for transfers between devices, on_device(): lax.psum(own_qkv.astype(jnp.bfloat16), 'replica').astype(jnp.float32)  83.1 us
    reduce_scatter x1, waiting for transfers between devices, on_device(): lax.psum_scatter(jnp.dot(normed_one.T, grad_proj, preferred_element_type=...  45.9 us
    all_gather x1, waiting for transfers between devices, on_device(): group_cot = lax.all_gather(cot_rows, 'shard', axis=0, tiled=True)  45.5 us
    all_gather x1, waiting for transfers between devices, on_device(): lax.all_gather(w_qkv, 'shard', axis=1, tiled=True)  30 us
    all_gather x1, waiting for transfers between devices, on_device(): group_rows = lax.all_gather(normed_two, 'shard', axis=0, tiled=True)  25.4 us
    all_gather x1, waiting for transfers between devices, on_device(): lax.all_gather(w_out, 'shard', axis=1, tiled=True)  24.7 us
    unnamed x105, local copies, waits for them, and re-layouts  21.8 us
  transfers between devices with their start and end apart: 9, of which 8 were waited for; matrix products, arithmetic and copies ran while one was open for 13% of the time, Pallas kernels for 0%

commit v1 on v0

--- a/solution.py
+++ b/solution.py
@@ -161,7 +161,14 @@
     hidden_out = (middle + branch_out).astype(jnp.bfloat16).reshape(hidden_in.shape)
     cot_rows = cotangent.reshape(row_total, D)
     cot_float = cot_rows.astype(jnp.float32)
-    group_cot = lax.all_gather(cot_rows, "shard", axis=0, tiled=True)
+    x = cot_rows
+    ways, here, step = (lax.axis_size("shard"), lax.axis_index("shard"), x.shape[0])
+    lengths = [n * ways if d == 0 else n for d, n in enumerate(x.shape)]
+    full = lax.dynamic_update_slice_in_dim(jnp.zeros(lengths, x.dtype), x, here * step, axis=0)
+    for far in range(1, ways):
+        x = lax.ppermute(x, "shard", [(d, (d + 1) % ways) for d in range(ways)])
+        full = lax.dynamic_update_slice_in_dim(full, x, (here - far) % ways * step, axis=0)
+    group_cot = full
     grad_act = jnp.dot(group_cot, w_down.T, preferred_element_type=jnp.float32)
     grad_up_b = (grad_act * silu_val).astype(jnp.bfloat16)
     grad_gate_b = (grad_act * up_pre * silu_slope).astype(jnp.bfloat16)

time: 494 us -> 460 us (0.931)
  waiting for transfers between devices: 264 us -> 223 us
  starting transfers between devices: 7.37 us -> 12.6 us
    all_gather x1 -> x0, waiting for transfers between devices: 45.5 us -> none  [on_device(): group_cot = lax.all_gather(cot_rows, 'shard', axis=0, tiled=True)]
    ppermute x0 -> x3, waiting for transfers between devices: none -> 27.7 us  [on_device(): x = lax.ppermute(x, 'shard', [(d, (d + 1) % ways) for d in range(ways)])]
    all_gather x1, waiting for transfers between devices: 25.4 us -> 0.01 us  [on_device(): group_rows = lax.all_gather(normed_two, 'shard', axis=0, tiled=True)]
    dynamic_update_slice x0 -> x4, local copies, waits for them, and re-layouts: none -> 13.5 us  [the longest x3 10.2 us: on_device(): lax.dynamic_update_slice_in_dim(full, x, (here - far) % ways * step, axis=0)]
    all_gather x1 -> x0, local copies, waits for them, and re-layouts: 9.42 us -> none  [on_device(): group_cot = lax.all_gather(cot_rows, 'shard', axis=0, tiled=True)]
    ppermute x0 -> x3, starting transfers between devices: none -> 5.97 us  [on_device(): x = lax.ppermute(x, 'shard', [(d, (d + 1) % ways) for d in range(ways)])]
    unnamed x105 -> x106, local copies, waits for them, and re-layouts: 21.8 us -> 20.9 us
  transfers between devices with their start and end apart: 9 -> 11, of which waited for: 8 -> 9; matrix products, arithmetic and copies ran while one was open for 13% -> 14% of each run, Pallas kernels for 0% -> 0%
where the time goes in v1:
time: 460 us; the launch traced here: 459 us
  waiting for transfers between devices  223 us (48%)
  blocking collectives  98.7 us (21%)
  matrix products  45.7 us (10%)
  local copies, waits for them, and re-layouts  40 us (9%)
  other arithmetic  22.2 us (5%)
  between operations  16.8 us (4%)
  starting transfers between devices  12.6 us (3%)
    unnamed x3, blocking collectives  83.6 us
    psum x1, waiting for transfers between devices, on_device(): lax.psum(own_qkv.astype(jnp.bfloat16), 'replica').astype(jnp.float32)  83 us
    reduce_scatter x1, waiting for transfers between devices, on_device(): lax.psum_scatter(jnp.dot(normed_one.T, grad_proj, preferred_element_type=...  45.9 us
    all_gather x1, waiting for transfers between devices, on_device(): lax.all_gather(w_qkv, 'shard', axis=1, tiled=True)  31.8 us
    ppermute x3, waiting for transfers between devices, on_device(): x = lax.ppermute(x, 'shard', [(d, (d + 1) % ways) for d in range(ways)])  27.7 us
    all_gather x1, waiting for transfers between devices, on_device(): lax.all_gather(w_out, 'shard', axis=1, tiled=True)  24.7 us
    unnamed x106, local copies, waits for them, and re-layouts  20.9 us
    psum x1, blocking collectives, on_device(): lax.psum(own_gain_a.astype(jnp.bfloat16), 'replica').astype(jnp.float32)  15.1 us
  transfers between devices with their start and end apart: 11, of which 9 were waited for; matrix products, arithmetic and copies ran while one was open for 14% of the time, Pallas kernels for 0%

profile of v1, /device:TPU:0, one launch (start us, length us, event | category | flops | bytes accessed | tf_op | source)
XLA Modules:
  0.0 458.5 jit_solution(6219891576613478770)
XLA Ops:
  8.0 2.0 copy.49
  12.1 11.5 %all-reduce.11 = (bf16[960]{0:T(1024)(128)(2,1)S(1)}, bf16[960]{0:T(1024)(128)(2,1)S(1)}) all-reduce(bf16[960]{0:T(1024)(128)(2,1)S(1)} %dynamic-update-slice, bf16[960]{0:T(1024)(128)(2,1)S(1)} %dynamic-update-slice.1), channel_id=1, replica_groups=mesh['shard'=4,'replica'=8] {'shard'}, use_global_device_ids=true, to_apply=%add | all-reduce | flops 1920 | bytes 7680
  25.1 0.7 fusion.48
  25.8 31.8 %all-gather.5.cloned.1.call-done = bf16[960,1600]{0,1:T(8,128)(2,1)} async-done(((bf16[960,400]{0,1:T(8,128)(2,1)}), bf16[960,1600]{0,1:T(8,128)(2,1)}) %all-gather.5.cloned.1.call-update) | async-done | bytes 3072016 | tf_op jit(solution)/shard_map/all_gather | solution.py:133
  57.6 3.2 fusion.51
  61.1 0.8 copy.44
  61.9 0.9 copy.45
  63.1 1.1 slice_negate_fusion.3
  64.2 1.1 fusion.49
  67.5 1.1 copy-done.2
  69.4 24.7 %all-gather.7.cloned.1.call-done = bf16[960,960]{0,1:T(8,128)(2,1)} async-done(((bf16[960,240]{0,1:T(8,128)(2,1)}), bf16[960,960]{0,1:T(8,128)(2,1)}) %all-gather.7.cloned.1.call-update) | async-done | bytes 1843216 | tf_op jit(solution)/shard_map/all_gather | solution.py:134
  94.2 2.4 multiply_reduce_fusion.1
  96.6 0.9 fusion.40
  97.6 1.5 collective-permute-start
  99.1 14.0 %collective-permute-done = bf16[212,960]{1,0:T(8,128)(2,1)S(1)} collective-permute-done((bf16[212,960]{1,0:T(8,128)(2,1)S(1)}, bf16[212,960]{1,0:T(8,128)(2,1)S(1)}, u32[]{:S(2)}, u32[]{:S(2)}) %collective-permute-start) | collective-permute-done | bytes 407072 | tf_op jit(solution)/shard_map/ppermute | solution.py:169
  113.1 0.8 copy-done.27
  113.8 1.9 collective-permute-start.1
  115.7 12.1 %collective-permute-done.1 = bf16[212,960]{1,0:T(8,128)(2,1)} collective-permute-done((bf16[212,960]{1,0:T(8,128)(2,1)S(1)}, bf16[212,960]{1,0:T(8,128)(2,1)}, u32[]{:S(2)}, u32[]{:S(2)}) %collective-permute-start.1) | collective-permute-done | bytes 407072 | tf_op jit(solution)/shard_map/ppermute | solution.py:169
  127.7 2.6 collective-permute-start.2
  130.3 1.4 broadcast_in_dim.12
  131.7 3.3 dynamic_update_slice.12
  135.1 3.3 dynamic_update_slice.13
  138.4 3.4 dynamic_update_slice.14
  141.8 1.7 collective-permute-done.2
  143.5 3.4 dynamic_update_slice.15
  147.0 2.8 reshape.175
  149.8 3.5 fusion.63
  153.3 1.5 fusion.62
  154.8 2.1 multiply_convert_fusion
  157.0 2.7 convolution_convert_fusion.2
  159.7 1.5 fusion.64
  161.3 2.8 add_convert_fusion
  164.0 63.2 %fusion.57 = (bf16[224,960]{1,0:T(8,128)(2,1)S(1)}, bf16[224,960]{1,0:T(8,128)(2,1)S(1)}) fusion(bf16[848,960]{1,0:T(8,128)(2,1)} %convolution_convert_fusion.2, bf16[848,960]{1,0:T(8,128)(2,1)} %add_convert_fusion), kind=kCustom, calls=%all-reduce-scatter.2 | all-reduce-scatter fusion | flops 1720321 | bytes 4116992
  227.3 1.3 collective-permute-start.4
  229.3 4.9 %collective-permute-start.3 = (bf16[36,960]{1,0:T(8,128)(2,1)S(1)}, bf16[36,960]{1,0:T(8,128)(2,1)S(1)}, u32[]{:S(2)}, u32[]{:S(2)}) collective-permute-start(bf16[36,960]{1,0:T(8,128)(2,1)S(1)} %slice.56), channel_id=1, source_target_pairs={{0,8},{8,16},{16,24},{1,9},{9,17},{17,25},{2,10},{10,18},{18,26},{... | collective-permute-start | bytes 207368
  234.2 0.9 concatenate.40
  236.2 0.8 concatenate.39
  237.1 2.6 fusion.26
  239.6 1.8 convolution_convert_fusion.1
  241.5 2.4 copy.63
  244.2 3.4 convolution_convert_fusion.6
  247.6 2.0 copy.50
  249.6 1.4 multiply_reduce_fusion
  251.0 2.1 fusion.4
  254.0 0.9 copy-done.9
  257.4 2.8 convolution_convert_fusion
  260.3 1.4 copy-done.13
  261.7 4.0 convolution_convert_fusion.3
  265.7 2.7 convolution_convert_fusion.4
  268.5 2.7 convolution_convert_fusion.5
  271.2 7.9 %reduce-scatter.11.cloned.1.call-done = bf16[240,960]{1,0:T(8,128)(2,1)} async-done(((bf16[960,960]{1,0:T(8,128)(2,1)}), bf16[240,960]{1,0:T(8,128)(2,1)}) %reduce-scatter.11.cloned.1.call-update) | async-done | bytes 460816
  279.1 2.0 copy.64
  281.1 45.9 %reduce-scatter.9.cloned.1.call-done = bf16[960,400]{0,1:T(8,128)(2,1)} async-done(((bf16[960,1600]{0,1:T(8,128)(2,1)}), bf16[960,400]{0,1:T(8,128)(2,1)}) %reduce-scatter.9.cloned.1.call-update) | async-done | bytes 768016 | tf_op jit(solution)/shard_map/reduce_scatter | solution.py:214
  328.2 3.1 fusion.39
  331.3 8.9 %all-reduce.10 = (bf16[960]{0:T(1024)(128)(2,1)S(1)}, bf16[960]{0:T(1024)(128)(2,1)S(1)}) all-reduce(bf16[960]{0:T(1024)(128)(2,1)S(1)} %get-tuple-element.38, bf16[960]{0:T(1024)(128)(2,1)S(1)} %get-tuple-element.36), channel_id=6, replica_groups=mesh['shard'=4,'replica'=8] {'shard'}, use_global_device_ids=true, to_apply=%region_17.18.clone | all-reduce | flops 1920 | bytes 7680
  340.4 15.1 %all-reduce.8 = (bf16[240]{0:T(256)(128)(2,1)S(1)}, bf16[240]{0:T(256)(128)(2,1)S(1)}) all-reduce(bf16[240]{0:T(256)(128)(2,1)S(1)} %dynamic-slice.7, bf16[240]{0:T(256)(128)(2,1)S(1)} %dynamic-slice.9), channel_id=1, replica_groups=mesh['shard'=4,'replica'=8] {'replica'}, use_global_device_ids=true, to_apply=%region_18.19 | all-reduce | flops 480 | bytes 1920 | tf_op jit(solution)/shard_map/psum | solution.py:243
  356.7 1.4 fusion.36
  358.1 1.8 copy.54
  359.9 83.0 %all-reduce.15.cloned.1.call-done = (bf16[960,400]{0,1:T(8,128)(2,1)}, bf16[960,240]{1,0:T(8,128)(2,1)}, bf16[960,640]{1,0:T(8,128)(2,1)}, bf16[960,640]{1,0:T(8,128)(2,1)}, bf16[640,960]{0,1:T(8,128)(2,1)}) async-done(((bf16[960,400]{0,1:T(8,128)(2,1)}, bf16[960,240]{1,0:T(8,128)(2,1)}, bf16[960,640]{1,0:T(8,128)(2,1)}, bf16[960,640]{1,0:T(8,128)(2,1)}, bf16[640,960]{0,1:T(8,128)(2,1)}), ...) | async-done | bytes 4915216 | tf_op jit(solution)/shard_map/psum | solution.py:238
  442.9 2.6 convert_element_type.183
  445.5 1.0 convert_element_type.185
  446.6 1.6 convert_element_type.187
  448.3 1.6 convert_element_type.189
  450.1 1.6 convert_element_type.191
  (145 shorter events, 14.4 us)
Async XLA Ops:
  7.2 147.6 %copy-start = (bf16[640,960]{0,1:T(8,128)(2,1)S(1)}, bf16[640,960]{0,1:T(8,128)(2,1)}, u32[]{:S(2)}) copy-start(bf16[640,960]{0,1:T(8,128)(2,1)} %param.19) | copy-start | bytes 3686404
  7.2 3.2 copy-start.33
  7.2 3.0 copy-start.35
  7.2 3.0 copy-start.5
  7.2 4.4 copy-start.38
  7.2 4.7 %copy-start.39 = (bf16[240]{0:T(256)(128)(2,1)S(1)}, bf16[240]{0:T(256)(128)(2,1)}, u32[]{:S(2)}) copy-start(bf16[240]{0:T(256)(128)(2,1)} %param.21) | copy-start | bytes 1444
  7.2 17.8 %copy-start.34 = (s32[1,212]{1,0:T(1,128)S(1)}, s32[1,212]{1,0:T(1,128)}, u32[]{:S(2)}) copy-start(s32[1,212]{1,0:T(1,128)} %param.13) | copy-start | bytes 2548
  7.3 50.3 %all-gather.5.cloned.1.call-start = ((), (), s32[]{:S(2)}) async-start(), calls=%async_computation.2 | async-start | bytes 4096000 | tf_op jit(solution)/shard_map/all_gather | solution.py:133
  8.0 86.2 %all-gather.7.cloned.1.call-start = ((), (), s32[]{:S(2)}) async-start(), calls=%async_computation.3 | async-start | bytes 2457600 | tf_op jit(solution)/shard_map/all_gather | solution.py:134
  10.1 136.9 %all-gather.9.cloned.1.call-start = ((), (), s32[]{:S(2)}) async-start(), calls=%async_computation.5 | async-start | bytes 2211840 | tf_op jit(solution)/shard_map/all_gather | solution.py:150
  63.1 2.3 copy-start.16
  63.1 2.3 copy-start.17
  65.3 0.7 copy-start.18
  65.4 0.8 copy-start.28
  66.2 0.8 copy-start.8
  67.0 1.7 copy-start.2
  67.0 1.7 copy-start.23
  69.4 170.2 %copy-start.10 = (bf16[5,64,3,212]{3,1,2,0:T(8,128)(2,1)}, bf16[5,64,3,212]{3,1,2,0:T(8,128)(2,1)S(1)}, u32[]{:S(2)}) copy-start(bf16[5,64,3,212]{3,1,2,0:T(8,128)(2,1)S(1)} %fusion.12) | copy-start | bytes 1221124
  96.6 1.0 copy-start.11
  97.5 181.6 %reduce-scatter.11.cloned.1.call-start = ((), (), s32[]{:S(2)}) async-start(), calls=%async_computation.6 | async-start | bytes 2457600
  97.6 15.5 %collective-permute-start = (bf16[212,960]{1,0:T(8,128)(2,1)S(1)}, bf16[212,960]{1,0:T(8,128)(2,1)S(1)}, u32[]{:S(2)}, u32[]{:S(2)}) collective-permute-start(bf16[212,960]{1,0:T(8,128)(2,1)S(1)} %bitcast.134), channel_id=1, source_target_pairs={{0,8},{8,16},{16,24},{24,0},{1,9},{9,17},{17,25},{25,1},{2,10},{10... | collective-permute-start | bytes 1221128 | tf_op jit(solution)/shard_map/ppermute | solution.py:169
  113.1 0.8 copy-start.27
  113.8 13.9 %collective-permute-start.1 = (bf16[212,960]{1,0:T(8,128)(2,1)S(1)}, bf16[212,960]{1,0:T(8,128)(2,1)}, u32[]{:S(2)}, u32[]{:S(2)}) collective-permute-start(bf16[212,960]{1,0:T(8,128)(2,1)S(1)} %collective-permute-done), channel_id=1, source_target_pairs={{0,8},{8,16},{16,24},{24,0},{1,9},{9,17},{17,25},{25,1},{2,10},{10... | collective-permute-start | bytes 1221128 | tf_op jit(solution)/shard_map/ppermute | solution.py:169
  127.7 15.8 %collective-permute-start.2 = (bf16[212,960]{1,0:T(8,128)(2,1)}, bf16[212,960]{1,0:T(8,128)(2,1)}, u32[]{:S(2)}, u32[]{:S(2)}) collective-permute-start(bf16[212,960]{1,0:T(8,128)(2,1)} %collective-permute-done.1), channel_id=1, source_target_pairs={{0,8},{8,16},{16,24},{24,0},{1,9},{9,17},{17,25},{25,1},{2,10},{10... | collective-permute-start | bytes 1221128 | tf_op jit(solution)/shard_map/ppermute | solution.py:169
  149.8 3.5 copy-start.14
  149.8 3.5 copy-start.36
  153.3 1.5 copy-start.12
  156.9 2.8 copy-start.44
  156.9 2.8 copy-start.42
  156.9 4.3 copy-start.40
  159.7 1.6 copy-start.37
  227.3 6.9 %collective-permute-start.4 = (bf16[36,960]{1,0:T(8,128)(2,1)S(1)}, bf16[36,960]{1,0:T(8,128)(2,1)S(1)}, u32[]{:S(2)}, u32[]{:S(2)}) collective-permute-start(bf16[36,960]{1,0:T(8,128)(2,1)S(1)} %slice.57), channel_id=1, source_target_pairs={{0,8},{8,16},{16,24},{1,9},{9,17},{17,25},{2,10},{10,18},{18,26},{... | collective-permute-start | bytes 207368
  229.3 6.9 %collective-permute-start.3 = (bf16[36,960]{1,0:T(8,128)(2,1)S(1)}, bf16[36,960]{1,0:T(8,128)(2,1)S(1)}, u32[]{:S(2)}, u32[]{:S(2)}) collective-permute-start(bf16[36,960]{1,0:T(8,128)(2,1)S(1)} %slice.56), channel_id=1, source_target_pairs={{0,8},{8,16},{16,24},{1,9},{9,17},{17,25},{2,10},{10,18},{18,26},{... | collective-permute-start | bytes 207368
  243.9 83.1 %reduce-scatter.9.cloned.1.call-start = ((), (), s32[]{:S(2)}) async-start(), calls=%async_computation.4 | async-start | bytes 4096000 | tf_op jit(solution)/shard_map/reduce_scatter | solution.py:214
  244.2 6.7 %copy-start.3 = (f32[5,3,212,212]{2,3,1,0:T(8,128)S(1)}, f32[5,3,212,212]{2,3,1,0:T(8,128)}, u32[]{:S(2)}) copy-start(f32[5,3,212,212]{2,3,1,0:T(8,128)} %copy-done.2) | copy-start | bytes 8089924
  250.9 2.1 copy-start.19
  253.8 1.0 copy-start.9
  254.9 1.9 copy-start.24
  254.9 1.2 copy-start.4
  256.1 0.7 copy-start.31
  256.1 1.3 copy-start.6
  256.7 0.7 copy-start.29
  260.2 1.5 copy-start.13
  260.2 5.5 %copy-start.15 = (bf16[848,960]{1,0:T(8,128)(2,1)S(1)}, bf16[848,960]{1,0:T(8,128)(2,1)}, u32[]{:S(2)}) copy-start(bf16[848,960]{1,0:T(8,128)(2,1)} %reshape.175) | copy-start | bytes 4884484
  260.2 182.7 %all-reduce.15.cloned.1.call-start = ((), (), s32[]{:S(2)}) async-start(), calls=%async_computation.7 | async-start | bytes 9994240 | tf_op jit(solution)/shard_map/psum | solution.py:238
  261.7 4.0 copy-start.41
  265.7 2.7 copy-start.43
  327.0 1.0 copy-start.7
  327.0 1.2 copy-start.25
  327.0 1.2 copy-start.30
  327.0 1.3 copy-start.32
  442.9 2.6 copy-start.26
  442.9 3.6 copy-start.22
  446.6 1.8 copy-start.21
  448.3 1.8 copy-start.20
  449.9 1.8 copy-start.1
Sparse Core Ops, SparseCore 0:
  9.9 47.6 all-gather.4
  60.0 34.0 all-gather.6
  97.6 42.9 all-gather.8
  244.0 35.0 reduce-scatter.10
  282.0 44.9 reduce-scatter.8
  330.2 112.6 all-reduce.14
